TPU v7x, 32 devices: a whole 2x2x4 slice. The times are simulated.
32 devices in a mesh: batch: 8 (over y, x, core), mp: 4 (over z).
Axes of the slice: x: 2, y: 2, z: 4, core: 2. Of those that a mesh axis runs over, the one named last changes fastest.
Arguments:
- token_ids: int32 [8, 1536], P('batch'), may hold values from 0 to 30527
- segment_ids: int32 [8, 1536], P('batch'), may hold values from 0 to 8, never falling along the last dimension, each value on 1 to 1024 neighbouring positions
- row_of: int32 [30528], replicated, may hold values from 0 to 30527, each once
- query_count: int32 [1], replicated, may hold values from 16 to 32
- table: float32 [30528, 768], P('batch'), may hold values from -8 to 8
- qkv_weight: float32 [768, 3, 768], P('batch', None, 'mp'), may hold values from -0.21875 to 0.21875
- out_weight: float32 [768, 768], P('mp', 'batch'), may hold values from -0.875 to 0.875
- gate_up_weight: float32 [768, 2, 3072], P('batch', None, 'mp'), may hold values from -0.21875 to 0.21875
- down_weight: float32 [3072, 768], P('mp', 'batch'), may hold values from -0.109375 to 0.109375
- gains: float32 [2, 768], P(None, 'batch'), may hold values from 0.3 to 2.5
- table_m: float32 [30528, 768], P('batch'), may hold values from -0.0009765625 to 0.0009765625
- qkv_m: float32 [768, 3, 768], P('batch', None, 'mp'), may hold values from -0.0009765625 to 0.0009765625
- out_m: float32 [768, 768], P('mp', 'batch'), may hold values from -0.0009765625 to 0.0009765625
- gate_up_m: float32 [768, 2, 3072], P('batch', None, 'mp'), may hold values from -0.0009765625 to 0.0009765625
- down_m: float32 [3072, 768], P('mp', 'batch'), may hold values from -0.0009765625 to 0.0009765625
- gains_m: float32 [2, 768], P(None, 'batch'), may hold values from -0.0009765625 to 0.0009765625
- table_v: float32 [30528, 768], P('batch'), may hold values from 3.040972e-08 to 1.2163888e-07
- qkv_v: float32 [768, 3, 768], P('batch', None, 'mp'), may hold values from 3.040972e-08 to 1.2163888e-07
- out_v: float32 [768, 768], P('mp', 'batch'), may hold values from 3.040972e-08 to 1.2163888e-07
- gate_up_v: float32 [768, 2, 3072], P('batch', None, 'mp'), may hold values from 3.040972e-08 to 1.2163888e-07
- down_v: float32 [3072, 768], P('mp', 'batch'), may hold values from 3.040972e-08 to 1.2163888e-07
- gains_v: float32 [2, 768], P(None, 'batch'), may hold values from 3.040972e-08 to 1.2163888e-07
Outputs:
- loss: float32 [1], replicated
- grad_norm: float32 [1], replicated
- new_table: float32 [30528, 768], P('batch')
- new_qkv_weight: float32 [768, 3, 768], P('batch', None, 'mp')
- new_out_weight: float32 [768, 768], P('mp', 'batch')
- new_gate_up_weight: float32 [768, 2, 3072], P('batch', None, 'mp')
- new_down_weight: float32 [3072, 768], P('mp', 'batch')
- new_gains: float32 [2, 768], P(None, 'batch')
- clipped_table_grad: float32 [30528, 768], P('batch')
- new_qkv_m: float32 [768, 3, 768], P('batch', None, 'mp')
- new_out_m: float32 [768, 768], P('mp', 'batch')
- new_gate_up_m: float32 [768, 2, 3072], P('batch', None, 'mp')
- new_down_m: float32 [3072, 768], P('mp', 'batch')
- new_gains_m: float32 [2, 768], P(None, 'batch')
- new_table_v: float32 [30528, 768], P('batch')
- new_qkv_v: float32 [768, 3, 768], P('batch', None, 'mp')
- new_out_v: float32 [768, 768], P('mp', 'batch')
- new_gate_up_v: float32 [768, 2, 3072], P('batch', None, 'mp')
- new_down_v: float32 [3072, 768], P('mp', 'batch')
- new_gains_v: float32 [2, 768], P(None, 'batch')
Inputs may be any that keep to these rules, and one draw needn't show every extreme that they name: `segment_ids`: in each row the ids never fall, every id 0 to 8 appears, id 8 marks padding, each segment has 1 to 1024 tokens and one has exactly 1024. A permutation: token t's embedding is table row row_of[t]. The first query_count queries count.
All inputs are finite; a program needn't handle non-finite values.
Results may differ from a plain program's by a relative error of at most 0.0075.
The roundings to bfloat16 on the way count: a program that leaves them out, or rounds other values in their place, can miss the bound.
Values may be sent and summed in bfloat16 or wider, within the bound.
A program may use at most 320 MiB of HBM per device.

v0:
```python
from functools import partial
import jax
import jax.numpy as jnp
from jax import lax
from jax.sharding import PartitionSpec as P

D = 768
HEAD_DIM = 64
SEGS = 8
peak_affinity = lax.Precision.HIGHEST
sharpness_divisor = 0.05
clip_limit = 1.0
step_number = 3.0
rates = (0.3, 0.02, 0.02, 0.02, 0.02, 0.3)
negative = -1e30


def positions(segment_row, segment_count):
    labels = jnp.arange(segment_count + 1, dtype=jnp.int32)
    member = (segment_row[:, None] == labels[None, :]).astype(jnp.int32)
    counts = jnp.sum(member, 0)
    starts = jnp.cumsum(counts) - counts
    first_index = jnp.sum(member * starts[None, :], 1)
    return (jnp.arange(segment_row.shape[0], dtype=jnp.int32) - first_index).astype(jnp.float32)


def rotate(values, places):
    half_dim = values.shape[-1] // 2
    freqs = jnp.power(1000.0, -2.0 * jnp.arange(half_dim, dtype=jnp.float32) / values.shape[-1])
    angles = places[:, None] * freqs[None, :]
    cosine = jnp.cos(angles)[:, None, :]
    sine = jnp.sin(angles)[:, None, :]
    former = values[..., :half_dim]
    latter = values[..., half_dim:]
    return jnp.concatenate([former * cosine - latter * sine, latter * cosine + former * sine], -1)


def layer_norm(values, gain):
    centred = values - jnp.mean(values, -1, keepdims=True)
    spread = jnp.mean(centred * centred, -1, keepdims=True)
    return centred * lax.rsqrt(spread + 1e-05) * gain


def swiglu(gate_up):
    return jax.nn.silu(gate_up[:, 0]) * gate_up[:, 1]


def contract(left, right, left_dim, right_dim):
    return lax.dot_general(
        left, right, (((left_dim,), (right_dim,)), ((), ())), preferred_element_type=jnp.float32
    )


def pool_rows(hidden, segment_ids):
    rows_dev, length = segment_ids.shape
    labels = jnp.arange(SEGS, dtype=jnp.int32)
    member = (segment_ids[:, None, :] == labels[None, :, None]).astype(jnp.float32)
    sums = jnp.einsum(
        "rsl,rld->rsd", member, hidden.reshape(rows_dev, length, -1), precision=peak_affinity
    )
    pooled = (sums / jnp.sum(member, -1, keepdims=True)).reshape(rows_dev * SEGS, -1)
    return pooled * lax.rsqrt(jnp.sum(pooled * pooled, -1, keepdims=True) + 1e-06)


def block_scores(query_block, key_row, segment_block, segment_row):
    scores = jnp.einsum(
        "qhd,khd->hqk", query_block, key_row, preferred_element_type=jnp.float32
    ) * HEAD_DIM ** (-0.5)
    same = segment_block[:, None] == segment_row[None, :]
    return jnp.where(same[None], scores, negative)


def attend(query, keys, values, segment_ids, width):
    rows_dev, length = segment_ids.shape
    per_row = length // width
    flat_segments = segment_ids.reshape(-1)

    def one_block(block):
        row_index = block // per_row
        query_block = lax.dynamic_slice_in_dim(query, block * width, width, 0)
        segment_block = lax.dynamic_slice_in_dim(flat_segments, block * width, width, 0)
        scores = block_scores(query_block, keys[row_index], segment_block, segment_ids[row_index])
        peak_score = jnp.max(scores, -1, keepdims=True)
        weights = jnp.exp(scores - peak_score)
        totals = jnp.sum(weights, -1, keepdims=True)
        probs = (weights / totals).astype(jnp.bfloat16)
        output = jnp.einsum(
            "hqk,khd->qhd", probs, values[row_index], preferred_element_type=jnp.float32
        )
        return (output, (peak_score + jnp.log(totals))[..., 0])

    outputs, log_totals = lax.map(one_block, jnp.arange(rows_dev * per_row, dtype=jnp.int32))
    return (outputs.reshape((rows_dev * length,) + outputs.shape[2:]), log_totals)


def attend_back(query, keys, values, segment_ids, log_totals, grad_out, width):
    rows_dev, length = segment_ids.shape
    per_row = length // width
    flat_segments = segment_ids.reshape(-1)
    factor = HEAD_DIM ** (-0.5)

    def one_block(carry, block):
        grad_keys, grad_values = carry
        row_index = block // per_row
        query_block = lax.dynamic_slice_in_dim(query, block * width, width, 0)
        segment_block = lax.dynamic_slice_in_dim(flat_segments, block * width, width, 0)
        grad_block = lax.dynamic_slice_in_dim(grad_out, block * width, width, 0)
        scores = block_scores(query_block, keys[row_index], segment_block, segment_ids[row_index])
        probs = jnp.exp(scores - log_totals[block][..., None])
        grad_probs = jnp.einsum(
            "qhd,khd->hqk", grad_block, values[row_index], preferred_element_type=jnp.float32
        )
        inner = jnp.sum(probs * grad_probs, -1, keepdims=True)
        grad_scores = (probs * (grad_probs - inner)).astype(jnp.bfloat16)
        grad_query = (
            jnp.einsum(
                "hqk,khd->qhd", grad_scores, keys[row_index], preferred_element_type=jnp.float32
            )
            * factor
        )
        key_term = (
            jnp.einsum("hqk,qhd->khd", grad_scores, query_block, preferred_element_type=jnp.float32)
            * factor
        )
        value_term = jnp.einsum(
            "hqk,qhd->khd",
            probs.astype(jnp.bfloat16),
            grad_block,
            preferred_element_type=jnp.float32,
        )
        return (
            (grad_keys.at[row_index].add(key_term), grad_values.at[row_index].add(value_term)),
            grad_query,
        )

    zeros = jnp.zeros(keys.shape, jnp.float32)
    (grad_keys, grad_values), grad_query = lax.scan(
        one_block, (zeros, zeros), jnp.arange(rows_dev * per_row, dtype=jnp.int32)
    )
    return (grad_query.reshape((rows_dev * length,) + grad_query.shape[2:]), grad_keys, grad_values)


def adam_update(weight, grad, first, second, rate):
    first = 0.5 * first + 0.5 * grad
    second = 0.5 * second + 0.5 * grad * grad
    correction = 1.0 - 0.5**step_number
    weight = weight - rate * (
        first / correction / (jnp.sqrt(second / correction) + 1e-08) + 0.01 * weight
    )
    return (weight, first, second)


def local(
    token_ids,
    segment_ids,
    row_of,
    query_count,
    table,
    qkv_weight,
    out_weight,
    gate_up_weight,
    down_weight,
    gains,
    table_m,
    qkv_m,
    out_m,
    gate_up_m,
    down_m,
    gains_m,
    table_v,
    qkv_v,
    out_v,
    gate_up_v,
    down_v,
    gains_v,
):
    local_width = table.shape[1] // lax.axis_size("mp")
    column = lax.axis_index("mp") * local_width
    table_cols = lax.dynamic_slice_in_dim(table, column, local_width, 1)
    low_table, w_qkv, w_out, w_gu, w_down, gain_low = (
        lax.all_gather(table_cols.astype(jnp.bfloat16), "batch", axis=0, tiled=True),
        lax.all_gather(qkv_weight.astype(jnp.bfloat16), "batch", axis=0, tiled=True),
        lax.all_gather(out_weight.astype(jnp.bfloat16), "batch", axis=1, tiled=True),
        lax.all_gather(gate_up_weight.astype(jnp.bfloat16), "batch", axis=0, tiled=True),
        lax.all_gather(down_weight.astype(jnp.bfloat16), "batch", axis=1, tiled=True),
        lax.all_gather(gains.astype(jnp.bfloat16), "batch", axis=1, tiled=True),
    )
    gain = gain_low.astype(jnp.float32)
    rows_dev, length = token_ids.shape
    tokens = rows_dev * length
    width = min(512, length)
    heads_local = w_qkv.shape[2] // HEAD_DIM
    ff_local = w_gu.shape[2]
    table_rows = row_of[token_ids.reshape(-1)]
    x_zero = lax.all_gather(low_table[table_rows], "mp", axis=1, tiled=True)
    places = jax.vmap(partial(positions, segment_count=SEGS))(segment_ids).reshape(-1)
    qkv = jnp.dot(x_zero, w_qkv.reshape(D, -1), preferred_element_type=jnp.float32).reshape(
        tokens, 3, heads_local, HEAD_DIM
    )
    query = rotate(qkv[:, 0], places).astype(jnp.bfloat16)
    keys = (
        rotate(qkv[:, 1], places)
        .astype(jnp.bfloat16)
        .reshape(rows_dev, length, heads_local, HEAD_DIM)
    )
    values = qkv[:, 2].astype(jnp.bfloat16).reshape(rows_dev, length, heads_local, HEAD_DIM)
    attended, log_totals = attend(query, keys, values, segment_ids, width)
    attended_low = attended.reshape(tokens, -1).astype(jnp.bfloat16)
    attn_term = jnp.dot(attended_low, w_out, preferred_element_type=jnp.float32)
    attn = lax.psum(attn_term, "mp")
    hidden_one, first_back = jax.vjp(layer_norm, x_zero.astype(jnp.float32) + attn, gain[0])
    hidden_low = hidden_one.astype(jnp.bfloat16)
    gate_up = jnp.dot(hidden_low, w_gu.reshape(D, -1), preferred_element_type=jnp.float32).reshape(
        tokens, 2, ff_local
    )
    active, swiglu_back = jax.vjp(swiglu, gate_up)
    active_low = active.astype(jnp.bfloat16)
    mlp = lax.psum(jnp.dot(active_low, w_down, preferred_element_type=jnp.float32), "mp")
    hidden_two, second_back = jax.vjp(layer_norm, hidden_one + mlp, gain[1])
    embed, pool_back = jax.vjp(lambda hidden: pool_rows(hidden, segment_ids), hidden_two)
    batch_index = lax.axis_index("batch")
    half_count = lax.axis_size("batch") // 2
    texts = embed.shape[0]
    queries_all = half_count * texts
    everyone = lax.all_gather(embed, "batch", axis=0, tiled=True)
    question_vectors = everyone[:queries_all]
    passage_vectors = everyone[queries_all:]
    limit = query_count[0].astype(jnp.float32)
    labels = jnp.arange(queries_all, dtype=jnp.int32)
    weight_rows = (labels < query_count[0]).astype(jnp.float32) / limit
    affinity_scores = (
        jnp.dot(question_vectors, passage_vectors.T, precision=peak_affinity) / sharpness_divisor
    )
    target = (labels[:, None] == labels[None, :]).astype(jnp.float32)
    loss_value = jnp.sum(
        weight_rows
        * (jax.nn.logsumexp(affinity_scores, -1) - jnp.sum(affinity_scores * target, -1))
    )
    affinity_derivative = (jax.nn.softmax(affinity_scores, -1) - target) * weight_rows[:, None]
    grad_all = jnp.concatenate(
        [
            jnp.dot(affinity_derivative, passage_vectors, precision=peak_affinity)
            / sharpness_divisor,
            jnp.dot(affinity_derivative.T, question_vectors, precision=peak_affinity)
            / sharpness_divisor,
        ],
        0,
    )
    grad_embed = lax.dynamic_slice_in_dim(grad_all, batch_index * texts, texts, 0)
    (grad_two,) = pool_back(grad_embed)
    grad_second, grad_gain_two = second_back(grad_two)
    grad_mlp_low = grad_second.astype(jnp.bfloat16)
    grad_active = contract(grad_mlp_low, w_down, 1, 1)
    grad_down = contract(active_low, grad_mlp_low, 0, 0)
    (grad_gate_up,) = swiglu_back(grad_active)
    grad_gu_low = grad_gate_up.reshape(tokens, -1).astype(jnp.bfloat16)
    back_term = contract(grad_gu_low, w_gu.reshape(D, -1), 1, 1)
    grad_one = grad_second + lax.psum(back_term, "mp")
    grad_first, grad_gain_one = first_back(grad_one)
    grad_gu = contract(hidden_low, grad_gu_low, 0, 0)
    grad_attn_low = grad_first.astype(jnp.bfloat16)
    grad_attended = contract(grad_attn_low, w_out, 1, 1).astype(jnp.bfloat16)
    grad_out = contract(attended_low, grad_attn_low, 0, 0)
    grad_query, grad_keys, grad_values = attend_back(
        query,
        keys,
        values,
        segment_ids,
        log_totals,
        grad_attended.reshape(tokens, heads_local, HEAD_DIM),
        width,
    )
    _, rotate_back = jax.vjp(lambda inputs: rotate(inputs, places), qkv[:, 0])
    (grad_query_raw,) = rotate_back(grad_query)
    (grad_key_raw,) = rotate_back(grad_keys.reshape(tokens, heads_local, HEAD_DIM))
    grad_qkv_low = (
        jnp.stack(
            [grad_query_raw, grad_key_raw, grad_values.reshape(tokens, heads_local, HEAD_DIM)], 1
        )
        .reshape(tokens, -1)
        .astype(jnp.bfloat16)
    )
    grad_zero = grad_first + lax.psum(contract(grad_qkv_low, w_qkv.reshape(D, -1), 1, 1), "mp")
    grad_qkv = contract(x_zero, grad_qkv_low, 0, 0)
    grad_table = (
        jnp.zeros((low_table.shape[0], local_width), jnp.float32)
        .at[table_rows]
        .add(lax.dynamic_slice_in_dim(grad_zero, column, local_width, 1))
    )
    grad_gains = jnp.stack([grad_gain_one, grad_gain_two], 0)
    reduced = (
        lax.psum_scatter(grad_table, "batch", scatter_dimension=0, tiled=True),
        lax.psum_scatter(grad_qkv.reshape(D, 3, -1), "batch", scatter_dimension=0, tiled=True),
        lax.psum_scatter(grad_out, "batch", scatter_dimension=1, tiled=True),
        lax.psum_scatter(grad_gu.reshape(D, 2, -1), "batch", scatter_dimension=0, tiled=True),
        lax.psum_scatter(grad_down, "batch", scatter_dimension=1, tiled=True),
        lax.psum_scatter(grad_gains, "batch", scatter_dimension=1, tiled=True),
    )
    squares = sum((jnp.sum(part * part) for part in reduced[:5])) + jnp.sum(
        reduced[5] * reduced[5]
    ) / lax.axis_size("mp")
    table_full = lax.all_gather(reduced[0], "mp", axis=1, tiled=True)
    total_squares = lax.psum(squares, ("batch", "mp"))
    grad_norm = jnp.sqrt(total_squares)
    scale = clip_limit / jnp.maximum(grad_norm, clip_limit)
    olds = (table, qkv_weight, out_weight, gate_up_weight, down_weight, gains)
    grads_all = (table_full,) + tuple(reduced[1:])
    firsts = (table_m, qkv_m, out_m, gate_up_m, down_m, gains_m)
    seconds = (table_v, qkv_v, out_v, gate_up_v, down_v, gains_v)
    updated = [
        adam_update(weight_old, grad_part * scale, first_old, second_old, rate)
        for weight_old, grad_part, first_old, second_old, rate in zip(
            olds, grads_all, firsts, seconds, rates
        )
    ]
    clipped_table = table_full * scale
    loss = loss_value.reshape(1)
    return (
        loss,
        grad_norm.reshape(1),
        updated[0][0],
        updated[1][0],
        updated[2][0],
        updated[3][0],
        updated[4][0],
        updated[5][0],
        clipped_table,
        updated[1][1],
        updated[2][1],
        updated[3][1],
        updated[4][1],
        updated[5][1],
        updated[0][2],
        updated[1][2],
        updated[2][2],
        updated[3][2],
        updated[4][2],
        updated[5][2],
    )


def solution(mesh):
    placed = (
        P("batch", None),
        P("batch", None),
        P(),
        P(),
        P("batch", None),
        P("batch", None, "mp"),
        P("mp", "batch"),
        P("batch", None, "mp"),
        P("mp", "batch"),
        P(None, "batch"),
        P("batch", None),
        P("batch", None, "mp"),
        P("mp", "batch"),
        P("batch", None, "mp"),
        P("mp", "batch"),
        P(None, "batch"),
        P("batch", None),
        P("batch", None, "mp"),
        P("mp", "batch"),
        P("batch", None, "mp"),
        P("mp", "batch"),
        P(None, "batch"),
    )
    return jax.shard_map(
        local,
        mesh=mesh,
        in_specs=placed,
        out_specs=(
            P(),
            P(),
            P("batch", None),
            P("batch", None, "mp"),
            P("mp", "batch"),
            P("batch", None, "mp"),
            P("mp", "batch"),
            P(None, "batch"),
            P("batch", None),
            P("batch", None, "mp"),
            P("mp", "batch"),
            P("batch", None, "mp"),
            P("mp", "batch"),
            P(None, "batch"),
            P("batch", None),
            P("batch", None, "mp"),
            P("mp", "batch"),
            P("batch", None, "mp"),
            P("mp", "batch"),
            P(None, "batch"),
        ),
        check_vma=False,
    )
```

profile of v0, /device:TPU:0, one launch (start us, length us, event | category | flops | bytes accessed | tf_op | source)
XLA Modules:
  0.0 1895.6 jit_solution(3074774490312549609)
XLA Ops:
  7.3 12.4 copy.141
  31.4 63.1 %all-gather.17.cloned.1.call-done = bf16[8,3816,192]{1,2,0:T(8,128)(2,1)} async-done(((bf16[1,3816,192]{1,2,0:T(8,128)(2,1)}), bf16[8,3816,192]{1,2,0:T(8,128)(2,1)}) %all-gather.17.cloned.1.call-update) | async-done | bytes 11722768 | tf_op jit(solution)/shard_map/all_gather | solution.py:181
  94.5 18.1 copy.142
  112.6 11.2 gather_fusion.1
  126.6 13.2 all_gather.29
  151.9 23.6 %all-gather.15.cloned.1.call-done = bf16[1536,768]{0,1:T(8,128)(2,1)} async-done(((bf16[1536,192]{0,1:T(8,128)(2,1)}), bf16[1536,768]{0,1:T(8,128)(2,1)}) %all-gather.15.cloned.1.call-update) | async-done | bytes 2359312 | tf_op jit(solution)/shard_map/all_gather | solution.py:195
  179.8 33.9 %while.31 = (s32[]{:T(128)}, bf16[3,512,3,64]{1,3,2,0:T(8,128)(2,1)}, f32[3,3,512]{2,1,0:T(4,128)S(1)}, s32[3]{0:T(128)S(1)}, s32[1536]{0:T(1024)S(1)}, /*index=...) while((s32[]{:T(128)}, ...), condition=%wide.region_6.7_spmd, body=%wide.region_3.6_spmd.sunk | while | flops 633076224 | bytes 38029568 | solution.py:92
  232.6 156.8 %all-reduce.11.cloned.1.call-done = f32[1536,768]{0,1:T(8,128)} async-done(((f32[1536,768]{0,1:T(8,128)}), f32[1536,768]{0,1:T(8,128)}) %all-reduce.11.cloned.1.call-update) | async-done | bytes 4718608 | tf_op jit(solution)/shard_map/psum | solution.py:210
  421.9 171.2 %all-reduce.13.cloned.1.call-done = f32[1536,768]{0,1:T(8,128)} async-done(((f32[1536,768]{0,1:T(8,128)}), f32[1536,768]{0,1:T(8,128)}) %all-reduce.13.cloned.1.call-update) | async-done | bytes 4718608 | tf_op jit(solution)/shard_map/psum | solution.py:218
  601.2 9.5 all_gather.34
  633.7 169.7 %all-reduce.15.cloned.1.call-done = f32[1536,768]{0,1:T(8,128)} async-done(((f32[1536,768]{0,1:T(8,128)}), f32[1536,768]{0,1:T(8,128)}) %all-reduce.15.cloned.1.call-update) | async-done | bytes 4718608 | tf_op jit(solution)/shard_map/psum | solution.py:258
  821.4 161.7 %while.32 = (s32[]{:T(128)}, f32[1,1536,3,64]{1,3,2,0:T(8,128)}, f32[1,1536,3,64]{1,3,2,0:T(8,128)S(1)}, f32[3,512,3,64]{1,0,3,2:T(4,128)}, s32[3]{0:T(128)S(1)}...) while((s32[]{:T(128)}, f32[1,1536,3,64]{1,3,2,0:T(8,128)}, ...), condition=%wide.region_29.30_spmd.clone, body=%wide.region_26.29_spmd.clone.sunk | while | flops 1534130688 | bytes 86367704 | solution.py:137
  839.3 9.4 multiply_convert_fusion.4
  893.0 9.4 multiply_convert_fusion.4
  993.0 171.1 %all-reduce.17.cloned.1.call-done = f32[1536,768]{0,1:T(8,128)} async-done(((f32[1536,768]{0,1:T(8,128)}), f32[1536,768]{0,1:T(8,128)}) %all-reduce.17.cloned.1.call-update) | async-done | bytes 4718608 | tf_op jit(solution)/shard_map/psum | solution.py:283
  1166.3 21.2 %scatter_custom_fusion = f32[30528,192]{1,0:T(8,128)} fusion(s32[1536]{0:T(1024)} %copy-done.49, f32[1536,192]{1,0:T(8,128)S(1)} %copy.157, f32[]{:T(128)} %constant.228.clone.1), kind=kCustom, calls=%fused_computation.51 | custom fusion | flops 294912 | bytes 23446016 | tf_op jit(solution)/shard_map/scatter-add | solution.py:288
  1201.7 15.3 fusion.50
  1224.7 151.4 %reduce-scatter.11.cloned.1.call-done = f32[3816,192]{1,0:T(8,128)} async-done(((f32[30528,192]{1,0:T(8,128)}), f32[3816,192]{1,0:T(8,128)}) %reduce-scatter.11.cloned.1.call-update) | async-done | bytes 2930704 | tf_op jit(solution)/shard_map/reduce_scatter | solution.py:292
  1381.2 12.6 copy.160
  1393.8 28.0 %reduce-scatter.17.cloned.1.call-done = f32[768,96]{0,1:T(8,128)} async-done(((f32[768,768]{0,1:T(8,128)}), f32[768,96]{0,1:T(8,128)}) %reduce-scatter.17.cloned.1.call-update) | async-done | bytes 294928 | tf_op jit(solution)/shard_map/reduce_scatter | solution.py:296
  1423.5 36.1 %reduce-scatter.21.cloned.1.call-done = f32[96,2]{1,0:T(8,128)} async-done(((f32[768,2]{1,0:T(8,128)}), f32[96,2]{1,0:T(8,128)}) %reduce-scatter.21.cloned.1.call-update) | async-done | bytes 784
  1461.8 36.2 %reduce-scatter.19.cloned.1.call-done = f32[96,192]{1,0:T(8,128)} async-done(((f32[768,192]{1,0:T(8,128)}), f32[96,192]{1,0:T(8,128)}) %reduce-scatter.19.cloned.1.call-update) | async-done | bytes 73744
  1499.6 56.7 %reduce-scatter.15.cloned.1.call-done = f32[96,2,768]{2,0,1:T(8,128)} async-done(((f32[768,2,768]{2,0,1:T(8,128)}), f32[96,2,768]{2,0,1:T(8,128)}) %reduce-scatter.15.cloned.1.call-update) | async-done | bytes 589840 | tf_op jit(solution)/shard_map/reduce_scatter | solution.py:295
  1558.1 44.5 %reduce-scatter.13.cloned.1.call-done = f32[96,3,192]{2,0,1:T(8,128)} async-done(((f32[768,3,192]{2,0,1:T(8,128)}), f32[96,3,192]{2,0,1:T(8,128)}) %reduce-scatter.13.cloned.1.call-update) | async-done | bytes 221200 | tf_op jit(solution)/shard_map/reduce_scatter | solution.py:293
  1611.3 13.3 copy.158
  1624.7 53.5 %psum.39 = f32[]{:T(128)} all-reduce(f32[]{:T(128)S(6)} %add.324), channel_id=1, replica_groups=mesh['batch'=8,'mp'=4] {'batch','mp'}, use_global_device_ids=true, to_apply=%region_46.47 | all-reduce | flops 1 | bytes 8 | tf_op jit(solution)/shard_map/psum | solution.py:303
  1687.7 123.4 %all-gather.13.cloned.1.call-done = f32[3816,768]{0,1:T(8,128)} async-done(((f32[3816,192]{0,1:T(8,128)}), f32[3816,768]{0,1:T(8,128)}) %all-gather.13.cloned.1.call-update) | async-done | bytes 11722768 | tf_op jit(solution)/shard_map/all_gather | solution.py:302
  1811.0 17.3 fusion.46
  1828.4 12.3 copy.169
  1840.7 22.2 %fusion.45 = f32[3816,768]{0,1:T(8,128)} fusion(f32[3816,768]{0,1:T(8,128)} %copy.141, f32[3816,768]{0,1:T(8,128)} %get-tuple-element.440, f32[3816,768]{0,1:T(8,128)} %copy.158, f32[3816,768]{0,1:T(8,128)} %copy.160), kind=kLoop, calls=%fused_computation.57 | loop fusion | flops 41029632 | bytes 58613760 | tf_op jit(solution)/shard_map/sub | solution.py:147
  1862.9 12.3 copy.167
  1875.3 12.4 copy.171
  (347 shorter events, 350.5 us)
Async XLA Ops:
  7.2 87.3 %all-gather.17.cloned.1.call-start = ((), (), s32[]{:S(2)}) async-start(), calls=%async_computation.18 | async-start | bytes 13271040 | tf_op jit(solution)/shard_map/all_gather | solution.py:181
  22.8 152.7 %all-gather.15.cloned.1.call-start = ((), (), s32[]{:S(2)}) async-start(), calls=%async_computation.17 | async-start | bytes 2949120 | tf_op jit(solution)/shard_map/all_gather | solution.py:195
  31.4 81.2 %copy-start.49 = (s32[1536]{0:T(1024)}, s32[1536]{0:T(1024)S(1)}, u32[]{:S(2)}) copy-start(s32[1536]{0:T(1024)S(1)} %fusion.104) | copy-start | bytes 18436
  124.8 103.5 %all-gather.9.cloned.1.call-start = ((), (), s32[]{:S(2)}) async-start(), calls=%async_computation.7 | async-start | bytes 2654208 | tf_op jit(solution)/shard_map/all_gather | solution.py:184
  125.7 263.7 %all-reduce.11.cloned.1.call-start = ((), (), s32[]{:S(2)}) async-start(), calls=%async_computation.6 | async-start | bytes 9437184 | tf_op jit(solution)/shard_map/psum | solution.py:210
  151.1 64.4 %copy-start.10 = (bf16[192,768]{0,1:T(8,128)(2,1)}, bf16[192,768]{0,1:T(8,128)(2,1)S(1)}, u32[]{:S(2)}) copy-start(bf16[192,768]{0,1:T(8,128)(2,1)S(1)} %all_gather.30) | copy-start | bytes 884740
  218.5 196.3 %all-gather.11.cloned.1.call-start = ((), (), s32[]{:S(2)}) async-start(), calls=%async_computation.8 | async-start | bytes 1327104 | tf_op jit(solution)/shard_map/all_gather | solution.py:185
  219.2 373.9 %all-reduce.13.cloned.1.call-start = ((), (), s32[]{:S(2)}) async-start(), calls=%async_computation.9 | async-start | bytes 9437184 | tf_op jit(solution)/shard_map/psum | solution.py:218
  228.3 585.8 %copy-start.45 = (f32[768]{0:T(1024)}, f32[768]{0:T(1024)S(1)}, u32[]{:S(2)}) copy-start(f32[768]{0:T(1024)S(1)} %get-tuple-element.396) | copy-start | bytes 9220
  393.4 420.7 %copy-start.41 = (f32[1536]{0:T(1024)}, f32[1536]{0:T(1024)S(1)}, u32[]{:S(2)}) copy-start(f32[1536]{0:T(1024)S(1)} %broadcast_multiply_fusion.3) | copy-start | bytes 18436
  393.9 420.1 %copy-start.43 = (f32[1536]{0:T(1024)}, f32[1536]{0:T(1024)S(1)}, u32[]{:S(2)}) copy-start(f32[1536]{0:T(1024)S(1)} %fusion.101) | copy-start | bytes 18436
  421.0 382.4 %all-reduce.15.cloned.1.call-start = ((), (), s32[]{:S(2)}) async-start(), calls=%async_computation.10 | async-start | bytes 9437184 | tf_op jit(solution)/shard_map/psum | solution.py:258
  617.5 185.9 %copy-start.47 = (f32[1536]{0:T(1024)}, f32[1536]{0:T(1024)S(1)}, u32[]{:S(2)}) copy-start(f32[1536]{0:T(1024)S(1)} %negate_multiply_fusion.1) | copy-start | bytes 18436
  633.2 530.8 %all-reduce.17.cloned.1.call-start = ((), (), s32[]{:S(2)}) async-start(), calls=%async_computation.11 | async-start | bytes 9437184 | tf_op jit(solution)/shard_map/psum | solution.py:283
  821.4 163.9 %copy-start.20 = (f32[1536,32]{0,1:T(8,128)S(1)}, f32[1536,32]{0,1:T(8,128)}, u32[]{:S(2)}) copy-start(f32[1536,32]{0,1:T(8,128)} %copy-done.19) | copy-start | bytes 589828
  992.9 383.2 %reduce-scatter.11.cloned.1.call-start = ((), (), s32[]{:S(2)}) async-start(), calls=%async_computation.12 | async-start | bytes 35168256 | tf_op jit(solution)/shard_map/reduce_scatter | solution.py:292
  1187.5 234.4 %reduce-scatter.17.cloned.1.call-start = ((), (), s32[]{:S(2)}) async-start(), calls=%async_computation.15 | async-start | bytes 2654208 | tf_op jit(solution)/shard_map/reduce_scatter | solution.py:296
  1194.9 264.7 %reduce-scatter.21.cloned.1.call-start = ((), (), s32[]{:S(2)}) async-start(), calls=%async_computation.20 | async-start | bytes 442368
  1196.0 302.0 %reduce-scatter.19.cloned.1.call-start = ((), (), s32[]{:S(2)}) async-start(), calls=%async_computation.19 | async-start | bytes 884736
  1201.7 354.7 %reduce-scatter.15.cloned.1.call-start = ((), (), s32[]{:S(2)}) async-start(), calls=%async_computation.14 | async-start | bytes 5308416 | tf_op jit(solution)/shard_map/reduce_scatter | solution.py:295
  1217.1 385.6 %reduce-scatter.13.cloned.1.call-start = ((), (), s32[]{:S(2)}) async-start(), calls=%async_computation.13 | async-start | bytes 2654208 | tf_op jit(solution)/shard_map/reduce_scatter | solution.py:293
  1224.7 586.4 %all-gather.13.cloned.1.call-start = ((), (), s32[]{:S(2)}) async-start(), calls=%async_computation.16 | async-start | bytes 14745600 | tf_op jit(solution)/shard_map/all_gather | solution.py:302
  1611.3 67.6 %copy-start.13 = (f32[96,2,768]{2,1,0:T(2,128)S(1)}, f32[96,2,768]{2,1,0:T(2,128)}, u32[]{:S(2)}) copy-start(f32[96,2,768]{2,1,0:T(2,128)} %param.37) | copy-start | bytes 1769476
  1611.3 67.6 %copy-start.14 = (f32[96,2,768]{2,0,1:T(8,128)S(1)}, f32[96,2,768]{2,0,1:T(8,128)}, u32[]{:S(2)}) copy-start(f32[96,2,768]{2,0,1:T(8,128)} %reduce-scatter.15.cloned.1.call-done) | copy-start | bytes 1769476
  1611.3 67.6 %copy-start.31 = (f32[96,2,768]{2,1,0:T(2,128)S(1)}, f32[96,2,768]{2,1,0:T(2,128)}, u32[]{:S(2)}) copy-start(f32[96,2,768]{2,1,0:T(2,128)} %param.43) | copy-start | bytes 1769476
  1611.3 67.6 %copy-start.32 = (f32[96,2,768]{2,1,0:T(2,128)S(1)}, f32[96,2,768]{2,1,0:T(2,128)}, u32[]{:S(2)}) copy-start(f32[96,2,768]{2,1,0:T(2,128)} %param.49) | copy-start | bytes 1769476
  1624.6 58.6 %copy-start.55 = (f32[2,96]{1,0:T(2,128)S(1)}, f32[2,96]{1,0:T(2,128)}, u32[]{:S(2)}) copy-start(f32[2,96]{1,0:T(2,128)} %param.45) | copy-start | bytes 2308
  1624.6 58.6 %copy-start.56 = (f32[2,96]{1,0:T(2,128)S(1)}, f32[2,96]{1,0:T(2,128)}, u32[]{:S(2)}) copy-start(f32[2,96]{1,0:T(2,128)} %param.51) | copy-start | bytes 2308
  1624.6 59.2 %copy-start.36 = (f32[192,96]{1,0:T(8,128)S(1)}, f32[192,96]{1,0:T(8,128)}, u32[]{:S(2)}) copy-start(f32[192,96]{1,0:T(8,128)} %param.36) | copy-start | bytes 221188
  1624.6 60.9 %copy-start.24 = (f32[768,96]{0,1:T(8,128)S(1)}, f32[768,96]{0,1:T(8,128)}, u32[]{:S(2)}) copy-start(f32[768,96]{0,1:T(8,128)} %param.38) | copy-start | bytes 884740
  1624.6 60.9 %copy-start.27 = (f32[768,96]{0,1:T(8,128)S(1)}, f32[768,96]{0,1:T(8,128)}, u32[]{:S(2)}) copy-start(f32[768,96]{0,1:T(8,128)} %reduce-scatter.17.cloned.1.call-done) | copy-start | bytes 884740
  1624.6 60.9 %copy-start.37 = (f32[768,96]{0,1:T(8,128)S(1)}, f32[768,96]{0,1:T(8,128)}, u32[]{:S(2)}) copy-start(f32[768,96]{0,1:T(8,128)} %param.44) | copy-start | bytes 884740
  (53 other events, 413.0 us)
Sparse Core Ops, SparseCore 0:
  22.9 71.4 all-gather.16
  125.0 50.4 all-gather.14
  178.0 27.8 all-gather.8
  218.6 170.7 all-reduce.10
  391.7 23.0 all-gather.10
  421.1 171.9 all-reduce.12
  633.3 170.0 all-reduce.14
  993.0 170.9 all-reduce.16
  1187.6 188.4 reduce-scatter.10
  1379.3 42.5 reduce-scatter.16
  1425.8 33.7 reduce-scatter.20
  1463.0 34.9 reduce-scatter.18
  1502.4 53.8 reduce-scatter.14
  1560.1 42.5 reduce-scatter.12
  1604.7 206.2 all-gather.12
where the time goes:
time: 1900 us
  waiting for transfers between devices  1240 us (65%)
  local copies, waits for them, and re-layouts  191 us (10%)
  matrix products  179 us (9%)
  other arithmetic  153 us (8%)
  blocking collectives  94.2 us (5%)
  between operations  21.7 us (1%)
    psum x1, waiting for transfers between devices, local(): lax.psum(jnp.dot(active_low, w_down, preferred_element_type=jnp.float32),...  171 us
    psum x1, waiting for transfers between devices, local(): lax.psum(contract(grad_qkv_low, w_qkv.reshape(D, -1), 1, 1), 'mp')  171 us
    psum x1, waiting for transfers between devices, local(): grad_one = grad_second + lax.psum(back_term, 'mp')  170 us
    psum x1, waiting for transfers between devices, local(): attn = lax.psum(attn_term, 'mp')  157 us
    reduce_scatter x1, waiting for transfers between devices, local(): lax.psum_scatter(grad_table, 'batch', scatter_dimension=0, tiled=True)  151 us
    all_gather x1, waiting for transfers between devices, local(): table_full = lax.all_gather(reduced[0], 'mp', axis=1, tiled=True)  123 us
    unnamed x132, local copies, waits for them, and re-layouts  102 us
    unnamed x17, waiting for transfers between devices  72.6 us
  transfers between devices with their start and end apart: 15, of which 14 were waited for; matrix products, arithmetic and copies ran while one was open for 8% of the time, Pallas kernels for 0%

commit v1 on v0

--- a/solution.py
+++ b/solution.py
@@ -299,7 +299,12 @@
     squares = sum((jnp.sum(part * part) for part in reduced[:5])) + jnp.sum(
         reduced[5] * reduced[5]
     ) / lax.axis_size("mp")
-    table_full = lax.all_gather(reduced[0], "mp", axis=1, tiled=True)
+    ring = [reduced[0]]
+    for hop in range(3):
+        ring.append(lax.ppermute(ring[-1], "mp", [(dev, (dev + 1) % 4) for dev in range(4)]))
+    table_full = jnp.roll(
+        jnp.concatenate(ring[::-1], axis=1), (lax.axis_index("mp") + 1) * ring[0].shape[1], axis=1
+    )
     total_squares = lax.psum(squares, ("batch", "mp"))
     grad_norm = jnp.sqrt(total_squares)
     scale = clip_limit / jnp.maximum(grad_norm, clip_limit)

time: 1900 us -> 1710 us (0.900)
  waiting for transfers between devices: 1240 us -> 1130 us
  local copies, waits for them, and re-layouts: 191 us -> 158 us
  matrix products: 179 us -> 149 us
    ppermute x0 -> x3, waiting for transfers between devices: none -> 127 us  [local(): lax.ppermute(ring[-1], 'mp', [(dev, (dev + 1) % 4) for dev in range(4)])]
    all_gather x1 -> x0, waiting for transfers between devices: 123 us -> none  [local(): table_full = lax.all_gather(reduced[0], 'mp', axis=1, tiled=True)]
    unnamed x132 -> x116, local copies, waits for them, and re-layouts: 102 us -> 26 us
    unnamed x17 -> x16, waiting for transfers between devices: 72.6 us -> 0.25 us
    reduce_scatter x1, waiting for transfers between devices: 28 us -> 0.01 us  [local(): lax.psum_scatter(grad_down, 'batch', scatter_dimension=1, tiled=True)]
    concatenate x0 -> x1, local copies, waits for them, and re-layouts: none -> 27.7 us  [local(): jnp.roll(jnp.concatenate(ring[::-1], axis=1), (lax.axis_index('mp') + 1)...]
    reduce_scatter x1, waiting for transfers between devices: 56.7 us -> 35.4 us  [local(): lax.psum_scatter(grad_gu.reshape(D, 2, -1), 'batch', scatter_dimension=0,...]
  transfers between devices with their start and end apart: 15 -> 17, of which waited for: 14 -> 12; matrix products, arithmetic and copies ran while one was open for 8% -> 8% of each run, Pallas kernels for 0% -> 0%
where the time goes in v1:
time: 1710 us; the launch traced here: 1700 us
  waiting for transfers between devices  1130 us (66%)
  local copies, waits for them, and re-layouts  158 us (9%)
  matrix products  149 us (9%)
  other arithmetic  146 us (9%)
  blocking collectives  80.6 us (5%)
  between operations  21.7 us (1%)
    psum x1, waiting for transfers between devices, local(): lax.psum(jnp.dot(active_low, w_down, preferred_element_type=jnp.float32),...  171 us
    psum x1, waiting for transfers between devices, local(): lax.psum(contract(grad_qkv_low, w_qkv.reshape(D, -1), 1, 1), 'mp')  171 us
    psum x1, waiting for transfers between devices, local(): grad_one = grad_second + lax.psum(back_term, 'mp')  170 us
    reduce_scatter x1, waiting for transfers between devices, local(): lax.psum_scatter(grad_table, 'batch', scatter_dimension=0, tiled=True)  159 us
    psum x1, waiting for transfers between devices, local(): attn = lax.psum(attn_term, 'mp')  156 us
    ppermute x3, waiting for transfers between devices, local(): lax.ppermute(ring[-1], 'mp', [(dev, (dev + 1) % 4) for dev in range(4)])  127 us
    all_gather x1, waiting for transfers between devices, local(): lax.all_gather(table_cols.astype(jnp.bfloat16), 'batch', axis=0, tiled=True)  62.5 us
    reduce_scatter x1, waiting for transfers between devices, local(): lax.psum_scatter(grad_qkv.reshape(D, 3, -1), 'batch', scatter_dimension=0...  44.5 us
  transfers between devices with their start and end apart: 17, of which 12 were waited for; matrix products, arithmetic and copies ran while one was open for 8% of the time, Pallas kernels for 0%

profile of v1, /device:TPU:0, one launch (start us, length us, event | category | flops | bytes accessed | tf_op | source)
XLA Modules:
  0.0 1704.7 jit_solution(17679098862150945151)
XLA Ops:
  13.2 8.4 gather_fusion
  21.7 62.5 %all-gather.14.cloned.1.call-done = bf16[8,3816,192]{1,2,0:T(8,128)(2,1)} async-done(((bf16[1,3816,192]{1,2,0:T(8,128)(2,1)}), bf16[8,3816,192]{1,2,0:T(8,128)(2,1)}) %all-gather.14.cloned.1.call-update) | async-done | bytes 11722768 | tf_op jit(solution)/shard_map/all_gather | solution.py:181
  84.2 18.0 %copy.140 = bf16[8,3816,192]{2,1,0:T(8,128)(2,1)} copy(bf16[8,3816,192]{1,2,0:T(8,128)(2,1)} %all-gather.14.cloned.1.call-done) | data formatting | bytes 23445504 | tf_op jit(solution)/shard_map/all_gather | solution.py:181
  102.3 11.2 gather_fusion.1
  116.4 9.5 all_gather.27
  126.0 13.1 all_gather.26
  140.8 24.5 %all-gather.12.cloned.1.call-done = bf16[1536,768]{0,1:T(8,128)(2,1)} async-done(((bf16[1536,192]{0,1:T(8,128)(2,1)}), bf16[1536,768]{0,1:T(8,128)(2,1)}) %all-gather.12.cloned.1.call-update) | async-done | bytes 2359312 | tf_op jit(solution)/shard_map/all_gather | solution.py:195
  169.3 33.8 %while.31 = (s32[]{:T(128)}, bf16[3,512,3,64]{1,3,2,0:T(8,128)(2,1)}, f32[3,3,512]{2,1,0:T(4,128)S(1)}, s32[3]{0:T(128)S(1)}, s32[1536]{0:T(1024)S(1)}, /*index=...) while((s32[]{:T(128)}, ...), condition=%wide.region_6.7_spmd, body=%wide.region_3.6_spmd.sunk | while | flops 633076224 | bytes 38029576 | solution.py:92
  211.0 8.9 all-gather.2
  224.3 155.7 %all-reduce.11.cloned.1.call-done = f32[1536,768]{0,1:T(8,128)} async-done(((f32[1536,768]{0,1:T(8,128)}), f32[1536,768]{0,1:T(8,128)}) %all-reduce.11.cloned.1.call-update) | async-done | bytes 4718608 | tf_op jit(solution)/shard_map/psum | solution.py:210
  395.9 9.5 all-gather.10.cloned.1.call-done
  411.8 171.2 %all-reduce.13.cloned.1.call-done = f32[1536,768]{0,1:T(8,128)} async-done(((f32[1536,768]{0,1:T(8,128)}), f32[1536,768]{0,1:T(8,128)}) %all-reduce.13.cloned.1.call-update) | async-done | bytes 4718608 | tf_op jit(solution)/shard_map/psum | solution.py:218
  591.1 9.5 all_gather.31
  623.2 169.7 %all-reduce.15.cloned.1.call-done = f32[1536,768]{0,1:T(8,128)} async-done(((f32[1536,768]{0,1:T(8,128)}), f32[1536,768]{0,1:T(8,128)}) %all-reduce.15.cloned.1.call-update) | async-done | bytes 4718608 | tf_op jit(solution)/shard_map/psum | solution.py:258
  810.8 133.5 %while.32 = (s32[]{:T(128)}, f32[1,1536,3,64]{1,3,2,0:T(8,128)S(1)}, f32[1,1536,3,64]{1,3,2,0:T(8,128)S(1)}, f32[3,512,3,64]{1,0,3,2:T(4,128)}, s32[3]{0:T(128)S...) while((s32[]{:T(128)}, ...), condition=%wide.region_29.30_spmd.clone, body=%wide.region_26.29_spmd.clone.sunk | while | flops 1534130688 | bytes 138272240 | solution.py:137
  827.0 9.4 multiply_convert_fusion.4
  846.7 8.6 dynamic_update_slice.22
  871.5 9.4 multiply_convert_fusion.4
  891.2 8.6 dynamic_update_slice.22
  916.0 9.4 multiply_convert_fusion.4
  935.7 8.6 dynamic_update_slice.22
  955.0 171.1 %all-reduce.17.cloned.1.call-done = f32[1536,768]{0,1:T(8,128)} async-done(((f32[1536,768]{0,1:T(8,128)}), f32[1536,768]{0,1:T(8,128)}) %all-reduce.17.cloned.1.call-update) | async-done | bytes 4718608 | tf_op jit(solution)/shard_map/psum | solution.py:283
  1128.3 21.2 %scatter_custom_fusion = f32[30528,192]{1,0:T(8,128)} fusion(s32[1536]{0:T(1024)} %copy-done.44, f32[1536,192]{1,0:T(8,128)S(1)} %copy.155, f32[]{:T(128)} %constant.245.clone.1), kind=kCustom, calls=%fused_computation.51 | custom fusion | flops 294912 | bytes 23446016 | tf_op jit(solution)/shard_map/scatter-add | solution.py:288
  1163.8 15.3 fusion.50
  1179.1 159.0 %reduce-scatter.11.cloned.1.call-done = f32[3816,192]{1,0:T(8,128)} async-done(((f32[30528,192]{1,0:T(8,128)}), f32[3816,192]{1,0:T(8,128)}) %reduce-scatter.11.cloned.1.call-update) | async-done | bytes 2930704 | tf_op jit(solution)/shard_map/reduce_scatter | solution.py:292
  1344.7 66.1 %collective-permute-done = f32[3816,192]{0,1:T(8,128)S(1)} collective-permute-done((f32[3816,192]{0,1:T(8,128)}, f32[3816,192]{0,1:T(8,128)S(1)}, u32[]{:S(2)}, u32[]{:S(2)}) %collective-permute-start) | collective-permute-done | bytes 2930720 | tf_op jit(solution)/shard_map/ppermute | solution.py:304
  1416.5 61.0 %collective-permute-done.1 = f32[3816,192]{0,1:T(8,128)} collective-permute-done((f32[3816,192]{0,1:T(8,128)S(1)}, f32[3816,192]{0,1:T(8,128)}, u32[]{:S(2)}, u32[]{:S(2)}) %collective-permute-start.1) | collective-permute-done | bytes 2930720 | tf_op jit(solution)/shard_map/ppermute | solution.py:304
  1483.0 35.4 %reduce-scatter.15.cloned.1.call-done = f32[96,2,768]{2,0,1:T(8,128)} async-done(((f32[768,2,768]{2,0,1:T(8,128)}), f32[96,2,768]{2,0,1:T(8,128)}) %reduce-scatter.15.cloned.1.call-update) | async-done | bytes 589840 | tf_op jit(solution)/shard_map/reduce_scatter | solution.py:295
  1520.2 44.5 %reduce-scatter.13.cloned.1.call-done = f32[96,3,192]{2,0,1:T(8,128)} async-done(((f32[768,3,192]{2,0,1:T(8,128)}), f32[96,3,192]{2,0,1:T(8,128)}) %reduce-scatter.13.cloned.1.call-update) | async-done | bytes 221200 | tf_op jit(solution)/shard_map/reduce_scatter | solution.py:293
  1573.3 39.6 %psum.39 = f32[]{:T(128)} all-reduce(f32[]{:T(128)S(6)} %add.337), channel_id=1, replica_groups=mesh['batch'=8,'mp'=4] {'batch','mp'}, use_global_device_ids=true, to_apply=%region_46.47 | all-reduce | flops 1 | bytes 8 | tf_op jit(solution)/shard_map/psum | solution.py:308
  1638.2 27.7 %concatenate.42 = f32[3816,1536]{1,0:T(8,128)} concatenate(f32[3816,192]{1,0:T(8,128)} %copy.157, f32[3816,192]{1,0:T(8,128)} %copy.158, f32[3816,192]{1,0:T(8,128)} %copy.159, f32[3816,192]{1,0:T(8,128)} %reduce-scatter.11.cloned.1.call-done, f32[3816,192]{1,0:T(8,128)} %copy.157, f32[3816,192]{1,0:T(8,128)} %copy.158, f32[3816,192]{1,0:T(8,128)} %copy.159, ...), dimensions={1} | concatenate | bytes 46891008 | tf_op jit(solution)/shard_map/jit(_roll_dynamic)/concatenate | solution.py:305
  1665.9 30.8 %fusion.45 = (f32[3816,768]{1,0:T(8,128)}, f32[3816,768]{1,0:T(8,128)}, f32[3816,768]{1,0:T(8,128)}) fusion(f32[3816,768]{1,0:T(8,128)} %param.34, f32[3816,768]{1,0:T(8,128)} %param.40, f32[3816,768]{1,0:T(8,128)} %param.46, f32[]{:T(128)S(6)} %div.197, f32[3816,1536]{1,0:T(8,128)} %concatenate.42, s32[]{:T(128)S(6)} %select_n.106), kind=kLoop, calls=%fused_computation.57 | loop fusion | flops 43960320 | bytes 82059272 | tf_op jit(solution)/shard_map/sub | solution.py:147
  (338 shorter events, 269.6 us)
Async XLA Ops:
  7.2 77.0 %all-gather.14.cloned.1.call-start = ((), (), s32[]{:S(2)}) async-start(), calls=%async_computation.17 | async-start | bytes 13271040 | tf_op jit(solution)/shard_map/all_gather | solution.py:181
  13.1 152.1 %all-gather.12.cloned.1.call-start = ((), (), s32[]{:S(2)}) async-start(), calls=%async_computation.16 | async-start | bytes 2949120 | tf_op jit(solution)/shard_map/all_gather | solution.py:195
  21.7 80.6 %copy-start.44 = (s32[1536]{0:T(1024)}, s32[1536]{0:T(1024)S(1)}, u32[]{:S(2)}) copy-start(s32[1536]{0:T(1024)S(1)} %fusion.103) | copy-start | bytes 18436
  114.6 105.5 %all-gather.8.cloned.1.call-start = ((), (), s32[]{:S(2)}) async-start(), calls=%async_computation.7 | async-start | bytes 2654208 | tf_op jit(solution)/shard_map/all_gather | solution.py:184
  115.4 264.6 %all-reduce.11.cloned.1.call-start = ((), (), s32[]{:S(2)}) async-start(), calls=%async_computation.6 | async-start | bytes 9437184 | tf_op jit(solution)/shard_map/psum | solution.py:210
  140.0 28.5 %copy-start.25 = (bf16[768,3,192]{0,2,1:T(8,128)(2,1)}, bf16[768,3,192]{0,2,1:T(8,128)(2,1)S(1)}, u32[]{:S(2)}) copy-start(bf16[768,3,192]{0,2,1:T(8,128)(2,1)S(1)} %copy.143) | copy-start | bytes 2654212
  140.7 28.1 %copy-start.18 = (f32[1536,32]{0,1:T(8,128)}, f32[1536,32]{0,1:T(8,128)S(1)}, u32[]{:S(2)}) copy-start(f32[1536,32]{0,1:T(8,128)S(1)} %get-tuple-element.487) | copy-start | bytes 589828
  140.8 28.1 %copy-start.19 = (f32[1536,32]{0,1:T(8,128)}, f32[1536,32]{0,1:T(8,128)S(1)}, u32[]{:S(2)}) copy-start(f32[1536,32]{0,1:T(8,128)S(1)} %get-tuple-element.488) | copy-start | bytes 589828
  209.1 171.0 %copy-start.13 = (bf16[1536,768]{0,1:T(8,128)(2,1)S(1)}, bf16[1536,768]{0,1:T(8,128)(2,1)}, u32[]{:S(2)}) copy-start(bf16[1536,768]{0,1:T(8,128)(2,1)} %all-gather.12.cloned.1.call-done) | copy-start | bytes 7077892
  209.1 196.3 %all-gather.10.cloned.1.call-start = ((), (), s32[]{:S(2)}) async-start(), calls=%async_computation.8 | async-start | bytes 1327104 | tf_op jit(solution)/shard_map/all_gather | solution.py:185
  211.0 372.0 %all-reduce.13.cloned.1.call-start = ((), (), s32[]{:S(2)}) async-start(), calls=%async_computation.9 | async-start | bytes 9437184 | tf_op jit(solution)/shard_map/psum | solution.py:218
  220.0 583.5 %copy-start.40 = (f32[768]{0:T(1024)}, f32[768]{0:T(1024)S(1)}, u32[]{:S(2)}) copy-start(f32[768]{0:T(1024)S(1)} %get-tuple-element.396) | copy-start | bytes 9220
  383.3 420.3 %copy-start.36 = (f32[1536]{0:T(1024)}, f32[1536]{0:T(1024)S(1)}, u32[]{:S(2)}) copy-start(f32[1536]{0:T(1024)S(1)} %broadcast_multiply_fusion.2) | copy-start | bytes 18436
  383.8 419.7 %copy-start.38 = (f32[1536]{0:T(1024)}, f32[1536]{0:T(1024)S(1)}, u32[]{:S(2)}) copy-start(f32[1536]{0:T(1024)S(1)} %fusion.100) | copy-start | bytes 18436
  410.9 382.0 %all-reduce.15.cloned.1.call-start = ((), (), s32[]{:S(2)}) async-start(), calls=%async_computation.10 | async-start | bytes 9437184 | tf_op jit(solution)/shard_map/psum | solution.py:258
  607.4 185.4 %copy-start.42 = (f32[1536]{0:T(1024)}, f32[1536]{0:T(1024)S(1)}, u32[]{:S(2)}) copy-start(f32[1536]{0:T(1024)S(1)} %negate_multiply_fusion.1) | copy-start | bytes 18436
  622.7 503.4 %all-reduce.17.cloned.1.call-start = ((), (), s32[]{:S(2)}) async-start(), calls=%async_computation.11 | async-start | bytes 9437184 | tf_op jit(solution)/shard_map/psum | solution.py:283
  955.0 383.2 %reduce-scatter.11.cloned.1.call-start = ((), (), s32[]{:S(2)}) async-start(), calls=%async_computation.12 | async-start | bytes 35168256 | tf_op jit(solution)/shard_map/reduce_scatter | solution.py:292
  1149.6 328.0 %reduce-scatter.17.cloned.1.call-start = ((), (), s32[]{:S(2)}) async-start(), calls=%async_computation.15 | async-start | bytes 2654208 | tf_op jit(solution)/shard_map/reduce_scatter | solution.py:296
  1157.0 322.2 %reduce-scatter.21.cloned.1.call-start = ((), (), s32[]{:S(2)}) async-start(), calls=%async_computation.19 | async-start | bytes 442368
  1158.0 323.3 %reduce-scatter.19.cloned.1.call-start = ((), (), s32[]{:S(2)}) async-start(), calls=%async_computation.18 | async-start | bytes 884736
  1163.7 354.7 %reduce-scatter.15.cloned.1.call-start = ((), (), s32[]{:S(2)}) async-start(), calls=%async_computation.14 | async-start | bytes 5308416 | tf_op jit(solution)/shard_map/reduce_scatter | solution.py:295
  1179.1 385.6 %reduce-scatter.13.cloned.1.call-start = ((), (), s32[]{:S(2)}) async-start(), calls=%async_computation.13 | async-start | bytes 2654208 | tf_op jit(solution)/shard_map/reduce_scatter | solution.py:293
  1343.2 67.6 %collective-permute-start = (f32[3816,192]{0,1:T(8,128)}, f32[3816,192]{0,1:T(8,128)S(1)}, u32[]{:S(2)}, u32[]{:S(2)}) collective-permute-start(f32[3816,192]{0,1:T(8,128)} %copy.156), channel_id=1, source_target_pairs={{0,1},{1,2},{2,3},{3,0},{4,5},{5,6},{6,7},{7,4},{8,9},{9,10},{10,1... | collective-permute-start | bytes 8792072 | tf_op jit(solution)/shard_map/ppermute | solution.py:304
  1410.9 66.7 %collective-permute-start.1 = (f32[3816,192]{0,1:T(8,128)S(1)}, f32[3816,192]{0,1:T(8,128)}, u32[]{:S(2)}, u32[]{:S(2)}) collective-permute-start(f32[3816,192]{0,1:T(8,128)S(1)} %collective-permute-done), channel_id=1, source_target_pairs={{0,1},{1,2},{2,3},{3,0},{4,5},{5,6},{6,7},{7,4},{8,9},{9,10},{10,1... | collective-permute-start | bytes 8792072 | tf_op jit(solution)/shard_map/ppermute | solution.py:304
  1477.5 155.7 %collective-permute-start.2 = (f32[3816,192]{0,1:T(8,128)}, f32[3816,192]{0,1:T(8,128)}, u32[]{:S(2)}, u32[]{:S(2)}) collective-permute-start(f32[3816,192]{0,1:T(8,128)} %collective-permute-done.1), channel_id=1, source_target_pairs={{0,1},{1,2},{2,3},{3,0},{4,5},{5,6},{6,7},{7,4},{8,9},{9,10},{10,1... | collective-permute-start | bytes 8792072 | tf_op jit(solution)/shard_map/ppermute | solution.py:304
  1570.0 49.7 %copy-start.49 = (f32[2,96]{1,0:T(2,128)S(1)}, f32[2,96]{1,0:T(2,128)}, u32[]{:S(2)}) copy-start(f32[2,96]{1,0:T(2,128)} %param.39) | copy-start | bytes 2308
  1570.0 49.7 %copy-start.50 = (f32[2,96]{1,0:T(2,128)S(1)}, f32[2,96]{1,0:T(2,128)}, u32[]{:S(2)}) copy-start(f32[2,96]{1,0:T(2,128)} %param.45) | copy-start | bytes 2308
  1570.0 49.7 %copy-start.51 = (f32[2,96]{1,0:T(2,128)S(1)}, f32[2,96]{1,0:T(2,128)}, u32[]{:S(2)}) copy-start(f32[2,96]{1,0:T(2,128)} %param.51) | copy-start | bytes 2308
  1570.0 50.3 %copy-start.31 = (f32[192,96]{1,0:T(8,128)S(1)}, f32[192,96]{1,0:T(8,128)}, u32[]{:S(2)}) copy-start(f32[192,96]{1,0:T(8,128)} %param.36) | copy-start | bytes 221188
  1570.0 52.0 %copy-start.21 = (f32[768,96]{0,1:T(8,128)S(1)}, f32[768,96]{0,1:T(8,128)}, u32[]{:S(2)}) copy-start(f32[768,96]{0,1:T(8,128)} %param.38) | copy-start | bytes 884740
  1665.9 30.8 %copy-start.1 = (s32[30528]{0:T(1024)S(1)}, s32[30528]{0:T(1024)}, u32[]{:S(2)}) copy-start(s32[30528]{0:T(1024)} %param.32) | copy-start | bytes 366340
  (50 other events, 303.6 us)
Sparse Core Ops, SparseCore 0:
  13.2 70.9 all-gather.13
  114.7 50.4 all-gather.11
  167.7 27.8 all-gather.7
  209.2 170.7 all-reduce.10
  382.3 23.0 all-gather.9
  411.0 171.9 all-reduce.12
  622.8 170.0 all-reduce.14
  955.1 170.9 all-reduce.16
  1149.6 188.4 reduce-scatter.10
  1341.4 42.4 reduce-scatter.16
  1387.8 33.8 reduce-scatter.20
  1425.0 34.9 reduce-scatter.18
  1464.4 53.9 reduce-scatter.14
  1522.1 42.4 reduce-scatter.12
